TPU v7x, 512 devices: a whole 4x8x8 slice. The times are simulated.
512 devices in a mesh: pipe: 8 (over y_lo, x), expert: 64 (over y_hi, z, core).
Axes of the slice: x: 4, y: 8 (y_hi: 4, y_lo: 2; y = y_hi * 2 + y_lo), z: 8, core: 2. Of those that a mesh axis runs over, the one named last changes fastest.
Arguments:
- state: bfloat16 [64, 8, 128, 2048], P('expert', 'pipe'), may hold values from -24 to 24
- query: bfloat16 [64, 8, 128, 2048], P('expert', 'pipe'), may hold values from -8 to 8
- enc_kv: bfloat16 [64, 256, 2, 2048], P('expert', 'pipe'), may hold values from -4 to 4
- gain: float32 [2048], replicated, may hold values from 0.1 to 1.9
- w_in: bfloat16 [2048, 24576], P(None, 'expert'), may hold values from -0.125 to 0.125
- w_out: bfloat16 [24576, 2048], P('expert'), may hold values from -0.109375 to 0.109375
- expert_id: int32 [64, 8, 128], P('expert', 'pipe'), may hold values from 0 to 7
- slot: int32 [64, 8, 128], P('expert', 'pipe'), may hold values from -1 to 23, as said below
- gate: float32 [64, 8, 128], P('expert', 'pipe'), may hold values from 0.3 to 1
Outputs:
- output: bfloat16 [64, 8, 128, 2048], P('expert', 'pipe')
Inputs may be any that keep to these rules, and one draw needn't show every extreme that they name: Within the 128 tokens of one source and sample, the tokens sent to one expert take slots 0, 1, 2, ... in token order until 24 are taken; later ones have slot -1. In every draw some expert is given 24 slotted tokens by every source and sample.
All inputs are finite; a program needn't handle non-finite values.
Results may differ from a plain program's by a relative error of at most 0.0055.
Values may be sent and summed in bfloat16 or wider, within the bound.
A program may use at most 128 MiB of HBM per device.

v0:
```python
import math
import jax
import jax.numpy as jnp
from jax import lax
from jax.sharding import PartitionSpec as P

HEADS = 16
HD = 128
WSPLIT = 8


def expert_ffn(slot_rows, w_in, w_out):
    senders, slots_here, width = slot_rows.shape
    flat_rows = slot_rows.reshape(senders * slots_here, width)
    activation = jnp.maximum(
        jnp.dot(flat_rows, w_in, preferred_element_type=jnp.float32), 0.0
    ).astype(jnp.bfloat16)
    partial_value = jnp.dot(activation, w_out, preferred_element_type=jnp.float32).astype(
        jnp.bfloat16
    )
    return partial_value.reshape(senders, slots_here, width)


def body(state, query, enc_kv, gain, w_in, w_out, expert_id, slot, gate):
    tokens = state.shape[2]
    width = state.shape[3]
    queries = query.reshape(tokens, HEADS, HD)
    scale = 1.0 / math.sqrt(HD)
    kv_piece = lax.all_gather(enc_kv, "pipe", axis=1, tiled=True)
    best_score = jnp.full((HEADS, tokens), -jnp.inf, jnp.float32)
    denominator = jnp.zeros((HEADS, tokens), jnp.float32)
    accumulated = jnp.zeros((HEADS, tokens, HD), jnp.float32)
    key_rows = kv_piece[0, :, 0].reshape(-1, HEADS, HD)
    value_rows = kv_piece[0, :, 1].reshape(-1, HEADS, HD)
    scores = (
        jnp.einsum("thd,lhd->htl", queries, key_rows, preferred_element_type=jnp.float32) * scale
    )
    new_best = jnp.max(scores, axis=2)
    factor = jnp.exp(best_score - new_best)
    raised = jnp.exp(scores - new_best[:, :, None])
    denominator = denominator * factor + jnp.sum(raised, axis=2)
    update = jnp.einsum(
        "htl,lhd->htd", raised.astype(jnp.bfloat16), value_rows, preferred_element_type=jnp.float32
    )
    best_score, denominator, accumulated = (
        new_best,
        denominator,
        accumulated * factor[:, :, None] + update,
    )
    attended = jnp.transpose(accumulated / denominator[:, :, None], (1, 0, 2)).reshape(
        tokens, width
    )
    hidden_state = state[0, 0].astype(jnp.float32) + attended
    mean_square = jnp.mean(hidden_state * hidden_state, axis=-1, keepdims=True)
    normed = (hidden_state * lax.rsqrt(mean_square + 1e-06) * gain).astype(jnp.bfloat16)
    experts = lax.axis_size("expert") // WSPLIT
    capacity = 3 * tokens // (2 * experts)
    flat_slot = jnp.where(slot[0, 0] >= 0, expert_id[0, 0] * capacity + slot[0, 0], -1)
    slot_ids = jnp.arange(experts * capacity, dtype=jnp.int32)
    selector = (slot_ids[:, None] == flat_slot[None, :]).astype(jnp.bfloat16)
    packed = jnp.dot(selector, normed, preferred_element_type=jnp.float32).astype(jnp.bfloat16)
    copies = jnp.broadcast_to(
        packed.reshape(experts, 1, capacity, width), (experts, WSPLIT, capacity, width)
    )
    copies = copies.reshape(experts * WSPLIT, capacity, width)
    partial_value = expert_ffn(
        lax.all_to_all(copies, "expert", split_axis=0, concat_axis=0, tiled=True), w_in, w_out
    )
    returned = lax.all_to_all(partial_value, "expert", split_axis=0, concat_axis=0, tiled=True)
    summed = jnp.sum(returned.reshape(experts, WSPLIT, capacity, width), axis=1, dtype=jnp.float32)
    summed = summed.reshape(experts * capacity, width)
    picked = jnp.take(summed, jnp.maximum(flat_slot, 0), axis=0)
    contribution = jnp.where((flat_slot >= 0)[:, None], gate[0, 0][:, None] * picked, 0.0)
    output = (hidden_state + contribution).astype(jnp.bfloat16)
    return output.reshape(1, 1, tokens, width)


def solution(mesh):
    return jax.shard_map(
        body,
        mesh=mesh,
        in_specs=(
            P("expert", "pipe", None, None),
            P("expert", "pipe", None, None),
            P("expert", "pipe", None, None),
            P(),
            P(None, "expert"),
            P("expert", None),
            P("expert", "pipe", None),
            P("expert", "pipe", None),
            P("expert", "pipe", None),
        ),
        out_specs=P("expert", "pipe", None, None),
        check_vma=False,
    )
```

profile of v0, /device:TPU:288, one launch (start us, length us, event | category | flops | bytes accessed | tf_op | source)
XLA Modules:
  0.0 509.5 jit_solution(5332171025868441447)
XLA Ops:
  6.5 0.0 copy-start
  6.5 0.0 copy-start.6
  6.5 0.0 copy-start.5
  6.5 0.0 all-gather.2.cloned.1.call-start
  6.5 0.7 all-gather.2.cloned.1.call-update
  7.3 1.1 copy.31
  8.4 2.2 copy.28
  10.7 0.0 copy-done.6
  10.7 0.0 copy-done.5
  10.7 46.0 %all-gather.2.cloned.1.call-done = bf16[1,256,2,2048]{3,2,0,1:T(2,128)(2,1)} async-done(((bf16[1,32,2,2048]{3,2,0,1:T(2,128)(2,1)}), bf16[1,256,2,2048]{3,2,0,1:T(2,128)(2,1)}) %all-gather.2.cloned.1.call-update) | async-done | bytes 2097168 | tf_op jit(solution)/shard_map/all_gather | solution.py:29
  56.6 6.8 %fusion.24 = (bf16[1,256,1,2048]{3,2,0,1:T(2,128)(2,1)}, bf16[1,256,1,2048]{3,2,0,1:T(2,128)(2,1)}) fusion(bf16[1,256,2,2048]{3,2,0,1:T(2,128)(2,1)} %all-gather.2.cloned.1.call-done), kind=kLoop, calls=%fused_computation.42 | loop fusion | bytes 4194304 | tf_op jit(solution)/shard_map/slice | solution.py:33
  63.4 4.5 copy.30
  68.0 0.5 multiply_reduce_fusion
  68.5 0.0 copy-start.1
  68.5 1.3 copy-done.1
  69.8 0.8 fusion.1
  70.6 5.8 %copy.25 = bf16[1,256,1,2048]{1,3,2,0:T(8,128)(2,1)} copy(bf16[1,256,1,2048]{3,2,0,1:T(2,128)(2,1)} %get-tuple-element.8) | data formatting | bytes 2097152 | tf_op jit(solution)/shard_map/slice | solution.py:34
  76.4 2.8 multiply_reduce_fusion.1
  79.2 0.0 copy-start.2
  79.2 0.0 copy-start.3
  79.2 1.3 copy.27
  80.5 0.0 copy-done.2
  80.5 0.0 copy-done.3
  80.5 1.7 convolution_convert_fusion.1
  82.2 0.8 broadcast_in_dim.54
  83.0 173.5 %all_to_all.10 = bf16[64,24,2048]{2,1,0:T(8,128)(2,1)} all-to-all(bf16[64,24,2048]{2,1,0:T(8,128)(2,1)S(1)} %bitcast.61), channel_id=1, replica_groups=mesh['pipe'=8,'expert'=64] {'expert'}, dimensions={0} | all-to-all | bytes 12582912 | tf_op jit(solution)/shard_map/all_to_all | solution.py:67
  256.5 0.0 copy-done
  256.5 10.9 %convolution_convert_fusion = bf16[1536,2048]{1,0:T(8,128)(2,1)} fusion(bf16[384,2048]{1,0:T(8,128)(2,1)S(1)} %copy-done, bf16[1536,2048]{1,0:T(8,128)(2,1)} %bitcast.63, bf16[2048,384]{1,0:T(8,128)(2,1)} %param.13), kind=kOutput, calls=%fused_computation.2 | convolution fusion | flops 4836163584 | bytes 15728640 | tf_op jit(solution)/shard_map/dot_general | solution.py:18
  267.4 12.9 %all-to-all-start.1 = ((bf16[64,24,2048]{2,1,0:T(8,128)(2,1)}), bf16[64,24,2048]{2,1,0:T(8,128)(2,1)}, u32[]{:S(2)}, u32[]{:S(2)}) async-start(bf16[64,24,2048]{2,1,0:T(8,128)(2,1)} %bitcast.62), calls=%async_computation.1 | async-start | bytes 12582912 | tf_op jit(solution)/shard_map/all_to_all | solution.py:69
  280.3 1.4 copy.26
  281.7 212.0 %all-to-all-done.1 = bf16[64,24,2048]{2,1,0:T(8,128)(2,1)} async-done(((bf16[64,24,2048]{2,1,0:T(8,128)(2,1)}), bf16[64,24,2048]{2,1,0:T(8,128)(2,1)}, u32[]{:S(2)}, u32[]{:S(2)}) %all-to-all-start.1) | async-done | bytes 6291488 | tf_op jit(solution)/shard_map/all_to_all | solution.py:69
  493.7 4.1 convert_reduce_fusion
  497.9 0.0 copy-start.4
  497.9 1.9 gather_fusion
  499.8 0.0 copy-done.4
  499.8 2.9 fusion.9
  (7 shorter events, 0.0 us)
Async XLA Ops:
  6.5 250.0 %copy-start = (bf16[384,2048]{1,0:T(8,128)(2,1)S(1)}, bf16[384,2048]{1,0:T(8,128)(2,1)}, u32[]{:S(2)}) copy-start(bf16[384,2048]{1,0:T(8,128)(2,1)} %param.14) | copy-start | bytes 4718596
  6.5 4.1 copy-start.6
  6.5 4.1 copy-start.5
  6.5 50.1 %all-gather.2.cloned.1.call-start = ((), (), s32[]{:S(2)}) async-start(), calls=%async_computation.2 | async-start | bytes 2359296 | tf_op jit(solution)/shard_map/all_gather | solution.py:29
  68.5 1.3 copy-start.1
  79.2 1.3 copy-start.2
  79.2 1.3 copy-start.3
  267.4 226.3 %all-to-all-start.1 = ((bf16[64,24,2048]{2,1,0:T(8,128)(2,1)}), bf16[64,24,2048]{2,1,0:T(8,128)(2,1)}, u32[]{:S(2)}, u32[]{:S(2)}) async-start(bf16[64,24,2048]{2,1,0:T(8,128)(2,1)} %bitcast.62), calls=%async_computation.1 | async-start | bytes 12582912 | tf_op jit(solution)/shard_map/all_to_all | solution.py:69
  497.9 1.9 copy-start.4
Sparse Core Ops, SparseCore 0:
  9.4 47.1 all-gather.1
where the time goes:
time: 510 us
  waiting for transfers between devices  259 us (51%)
  blocking collectives  174 us (34%)
  local copies, waits for them, and re-layouts  27.2 us (5%)
  matrix products  15.9 us (3%)
  between operations  13.5 us (3%)
  starting transfers between devices  12.9 us (3%)
  other arithmetic  7.85 us (2%)
    all_to_all x1, waiting for transfers between devices, body(): lax.all_to_all(partial_value, 'expert', split_axis=0, concat_axis=0, tile...  212 us
    all_to_all x1, blocking collectives, body(): lax.all_to_all(copies, 'expert', split_axis=0, concat_axis=0, tiled=True)  174 us
    all_gather x1, waiting for transfers between devices, body(): kv_piece = lax.all_gather(enc_kv, 'pipe', axis=1, tiled=True)  46 us
    all_to_all x1, starting transfers between devices, body(): lax.all_to_all(partial_value, 'expert', split_axis=0, concat_axis=0, tile...  12.9 us
    dot_general x1, matrix products, expert_ffn(): jnp.dot(activation, w_out, preferred_element_type=jnp.float32)  10.9 us
  transfers between devices with their start and end apart: 2, of which 2 were waited for; matrix products, arithmetic and copies ran while one was open for 1% of the time, Pallas kernels for 0%

commit v1 on v0

--- a/solution.py
+++ b/solution.py
@@ -26,7 +26,9 @@
     width = state.shape[3]
     queries = query.reshape(tokens, HEADS, HD)
     scale = 1.0 / math.sqrt(HD)
-    kv_piece = lax.all_gather(enc_kv, "pipe", axis=1, tiled=True)
+    kv_piece = jnp.concatenate(
+        lax.all_to_all(jnp.stack([enc_kv] * lax.axis_size("pipe")), "pipe", 0, 0), axis=1
+    )
     best_score = jnp.full((HEADS, tokens), -jnp.inf, jnp.float32)
     denominator = jnp.zeros((HEADS, tokens), jnp.float32)
     accumulated = jnp.zeros((HEADS, tokens, HD), jnp.float32)

time: 510 us -> 474 us (0.929)
  the two profiles are of different devices: /device:TPU:288 before, /device:TPU:36 now
where the time goes in v1:
time: 474 us; the launch traced here: 473 us
  waiting for transfers between devices  216 us (46%)
  blocking collectives  192 us (41%)
  starting transfers between devices  23.2 us (5%)
  local copies, waits for them, and re-layouts  17.5 us (4%)
  matrix products  16.9 us (4%)
  other arithmetic  7.85 us (2%)
    all_to_all x1, waiting for transfers between devices, body(): lax.all_to_all(partial_value, 'expert', split_axis=0, concat_axis=0, tile...  193 us
    all_to_all x1, blocking collectives, body(): lax.all_to_all(copies, 'expert', split_axis=0, concat_axis=0, tiled=True)  192 us
    all_to_all x1, waiting for transfers between devices, body(): lax.all_to_all(jnp.stack([enc_kv] * lax.axis_size('pipe')), 'pipe', 0, 0)  22.5 us
    all_to_all x1, starting transfers between devices, body(): lax.all_to_all(partial_value, 'expert', split_axis=0, concat_axis=0, tile...  18.2 us
    dot_general x1, matrix products, expert_ffn(): jnp.dot(activation, w_out, preferred_element_type=jnp.float32)  10.9 us
  transfers between devices with their start and end apart: 2, of which 2 were waited for; matrix products, arithmetic and copies ran while one was open for 1% of the time, Pallas kernels for 0%

profile of v1, /device:TPU:36, one launch (start us, length us, event | category | flops | bytes accessed | tf_op | source)
XLA Modules:
  0.0 473.2 jit_solution(10939798223697935386)
XLA Ops:
  0.0 0.0 copy-start
  0.0 1.2 copy.23
  1.2 1.6 stack.2
  2.7 0.0 copy-start.4
  2.7 0.0 copy-start.2
  2.7 5.0 %all-to-all-start = ((bf16[8,1,32,2,2048]{4,2,3,1,0:T(8,128)(2,1)}), bf16[8,1,32,2,2048]{4,2,3,1,0:T(8,128)(2,1)}, u32[]{:S(2)}, u32[]{:S(2)}) async-start(bf16[8,1,32,2,2048]{4,2,3,1,0:T(8,128)(2,1)} %stack.2), calls=%async_computation | async-start | bytes 4194304 | tf_op jit(solution)/shard_map/all_to_all | solution.py:30
  7.8 0.0 copy-start.7
  7.8 0.0 copy-start.8
  7.8 0.0 copy-done.4
  7.8 0.9 copy.33
  8.7 0.0 copy-done.2
  8.7 1.2 copy.31
  9.9 0.0 copy-done.7
  9.9 0.0 copy-done.8
  9.9 22.5 %all-to-all-done = bf16[8,1,32,2,2048]{4,2,3,1,0:T(8,128)(2,1)} async-done(((bf16[8,1,32,2,2048]{4,2,3,1,0:T(8,128)(2,1)}), bf16[8,1,32,2,2048]{4,2,3,1,0:T(8,128)(2,1)}, u32[]{:S(2)}, u32[]{:S(2)}) %all-to-all-start) | async-done | bytes 2097184 | tf_op jit(solution)/shard_map/all_to_all | solution.py:30
  32.3 1.7 copy.24
  34.1 1.4 fusion.24
  35.5 1.5 copy.25
  37.0 1.5 multiply_reduce_fusion
  38.5 0.0 copy-start.1
  38.6 0.0 copy-start.3
  38.6 1.3 copy-done.1
  39.9 0.8 fusion.1
  40.7 0.0 copy-done.3
  40.7 1.3 copy.28
  42.0 2.8 multiply_reduce_fusion.1
  44.8 0.0 copy-start.5
  44.8 1.3 copy.30
  46.1 0.0 copy-done.5
  46.1 1.7 convolution_convert_fusion.1
  47.8 0.8 broadcast_in_dim.54
  48.6 191.8 %all_to_all.15 = bf16[64,24,2048]{2,1,0:T(8,128)(2,1)} all-to-all(bf16[64,24,2048]{2,1,0:T(8,128)(2,1)S(1)} %bitcast.62), channel_id=1, replica_groups=mesh['pipe'=8,'expert'=64] {'expert'}, dimensions={0} | all-to-all | bytes 12582912 | tf_op jit(solution)/shard_map/all_to_all | solution.py:69
  240.4 0.0 copy-done
  240.4 10.9 %convolution_convert_fusion = bf16[1536,2048]{1,0:T(8,128)(2,1)} fusion(bf16[384,2048]{1,0:T(8,128)(2,1)S(1)} %copy-done, bf16[1536,2048]{1,0:T(8,128)(2,1)} %bitcast.65, bf16[2048,384]{1,0:T(8,128)(2,1)} %param.13), kind=kOutput, calls=%fused_computation.2 | convolution fusion | flops 4836163584 | bytes 15728640 | tf_op jit(solution)/shard_map/dot_general | solution.py:18
  251.3 18.2 %all-to-all-start.2 = ((bf16[64,24,2048]{2,1,0:T(8,128)(2,1)}), bf16[64,24,2048]{2,1,0:T(8,128)(2,1)}, u32[]{:S(2)}, u32[]{:S(2)}) async-start(bf16[64,24,2048]{2,1,0:T(8,128)(2,1)} %bitcast.64), calls=%async_computation.2 | async-start | bytes 12582912 | tf_op jit(solution)/shard_map/all_to_all | solution.py:71
  269.5 1.4 copy.29
  270.9 193.3 %all-to-all-done.2 = bf16[64,24,2048]{2,1,0:T(8,128)(2,1)} async-done(((bf16[64,24,2048]{2,1,0:T(8,128)(2,1)}), bf16[64,24,2048]{2,1,0:T(8,128)(2,1)}, u32[]{:S(2)}, u32[]{:S(2)}) %all-to-all-start.2) | async-done | bytes 6291488 | tf_op jit(solution)/shard_map/all_to_all | solution.py:71
  464.2 4.1 convert_reduce_fusion
  468.3 0.0 copy-start.6
  468.3 1.9 gather_fusion
  470.3 0.0 copy-done.6
  470.3 2.9 fusion.9
  (7 shorter events, 0.0 us)
Async XLA Ops:
  0.0 240.4 %copy-start = (bf16[384,2048]{1,0:T(8,128)(2,1)S(1)}, bf16[384,2048]{1,0:T(8,128)(2,1)}, u32[]{:S(2)}) copy-start(bf16[384,2048]{1,0:T(8,128)(2,1)} %param.14) | copy-start | bytes 4718596
  2.7 5.1 %copy-start.4 = (bf16[1,1,128,2048]{3,2,1,0:T(8,128)(2,1)S(1)}, bf16[1,1,128,2048]{3,2,1,0:T(8,128)(2,1)}, u32[]{:S(2)}) copy-start(bf16[1,1,128,2048]{3,2,1,0:T(8,128)(2,1)} %param.10) | copy-start | bytes 1572868
  2.7 6.0 %copy-start.2 = (bf16[1,1,128,2048]{3,2,1,0:T(8,128)(2,1)S(1)}, bf16[1,1,128,2048]{3,2,1,0:T(8,128)(2,1)}, u32[]{:S(2)}) copy-start(bf16[1,1,128,2048]{3,2,1,0:T(8,128)(2,1)} %param.9) | copy-start | bytes 1572868
  2.7 29.6 %all-to-all-start = ((bf16[8,1,32,2,2048]{4,2,3,1,0:T(8,128)(2,1)}), bf16[8,1,32,2,2048]{4,2,3,1,0:T(8,128)(2,1)}, u32[]{:S(2)}, u32[]{:S(2)}) async-start(bf16[8,1,32,2,2048]{4,2,3,1,0:T(8,128)(2,1)} %stack.2), calls=%async_computation | async-start | bytes 4194304 | tf_op jit(solution)/shard_map/all_to_all | solution.py:30
  7.8 2.1 copy-start.7
  7.8 2.1 copy-start.8
  38.5 1.3 copy-start.1
  38.6 2.1 copy-start.3
  44.8 1.3 copy-start.5
  251.3 212.9 %all-to-all-start.2 = ((bf16[64,24,2048]{2,1,0:T(8,128)(2,1)}), bf16[64,24,2048]{2,1,0:T(8,128)(2,1)}, u32[]{:S(2)}, u32[]{:S(2)}) async-start(bf16[64,24,2048]{2,1,0:T(8,128)(2,1)} %bitcast.64), calls=%async_computation.2 | async-start | bytes 12582912 | tf_op jit(solution)/shard_map/all_to_all | solution.py:71
  468.3 1.9 copy-start.6
